TPU v7x, 512 devices: a whole 4x8x8 slice. The times are simulated.
512 devices in a mesh: inst: 64 (over z_hi, x, y), tp: 8 (over z_lo, core).
Axes of the slice: x: 4, y: 8, z: 8 (z_hi: 2, z_lo: 4; z = z_hi * 4 + z_lo), core: 2. Of those that a mesh axis runs over, the one named last changes fastest.
Arguments:
- step_queries: bfloat16 [4, 512, 8192], P(None, 'inst', 'tp'), may hold values from -11 to 11
- step_keyvals: bfloat16 [4, 512, 8, 256], P(None, 'inst', 'tp'), may hold values from -9.5 to 9.5
- cache_pages: bfloat16 [8192, 16, 8, 256], P('inst', None, 'tp'), may hold values from -9.5 to 9.5
- block_table: int32 [512, 16], P('inst'), may hold values from 0 to 127, as said below
- context_len: int32 [512], replicated, may hold values from 1 to 256, as said below
- partner: int32 [64], replicated, may hold values from 0 to 63, as said below
- moved_slot: int32 [64], replicated, may hold values from 0 to 7
- prompt_queries: bfloat16 [32768, 8192], P(('inst', 'tp')), may hold values from -11 to 11
- prompt_keyvals: bfloat16 [32768, 8, 256], P(('inst', 'tp')), may hold values from -9.5 to 9.5
- prompt_target: int32 [32768, 1], replicated, may hold values from 0 to 63; in each aligned block of 64 rows (0 to 63, 64 to 127, ...) at most 2 rows name the same one
Outputs:
- decode_output: bfloat16 [4, 512, 8192], P(None, 'inst', 'tp')
- prefill_output: bfloat16 [65536, 8192], P('inst', 'tp')
Inputs may be any that keep to these rules, and one draw needn't show every extreme that they name: partner[partner[i]] = i, and i and partner[i] differ in exactly one bit. `block_table`: the 8 rows of one instance together name each of its 128 pages once. `context_len`: some request holds exactly 256 tokens. `prompt_target`: among the 64 rows of one device no instance is named more than 2 times.
All inputs are finite; a program needn't handle non-finite values.
Results may differ from a plain program's by a relative error of at most 0.0049.
Values may be sent and summed in bfloat16 or wider, within the bound.
No kernel may reach another device: no remote copies, remote signals or barrier semaphores. Data moves between devices by JAX's collectives and lax.ppermute only.
A program may use at most 64 MiB of HBM per device.

v0:
```python
import jax
import jax.numpy as jnp
from jax import lax
from jax.sharding import PartitionSpec as P


def swapped(array, axis, bit):
    return lax.ppermute(array, axis, [(i, i ^ 1 << bit) for i in range(lax.axis_size(axis))])


def masked_weights(scores, mask):
    shifted = jnp.where(mask, scores, jnp.float32(-1e30))
    top = jnp.max(shifted, axis=-1, keepdims=True)
    expo = jnp.where(mask, jnp.exp(shifted - top), jnp.float32(0.0))
    total = jnp.sum(expo, axis=-1, keepdims=True)
    total = jnp.where(total > 0, total, jnp.float32(1.0))
    return expo / total


def decode_block(queries, context, lengths, fresh):
    steps, count, width = queries.shape
    kv_heads = context.shape[2]
    head_dim = context.shape[3] // 2
    group = width // (kv_heads * head_dim)
    span = context.shape[1]
    scale = head_dim ** (-0.5)
    query = queries.reshape(steps, count, kv_heads, group, head_dim)
    past = (
        jnp.einsum(
            "trkgd,rckd->trkgc", query, context[..., :head_dim], preferred_element_type=jnp.float32
        )
        * scale
    )
    newer = (
        jnp.einsum(
            "trkgd,urkd->trkgu", query, fresh[..., :head_dim], preferred_element_type=jnp.float32
        )
        * scale
    )
    past_mask = (jnp.arange(span, dtype=jnp.int32)[None, :] < lengths[:, None])[
        None, :, None, None, :
    ]
    step_ids = jnp.arange(steps, dtype=jnp.int32)
    new_mask = (step_ids[None, :] <= step_ids[:, None])[:, None, None, None, :]
    mask = jnp.concatenate(
        [jnp.broadcast_to(past_mask, past.shape), jnp.broadcast_to(new_mask, newer.shape)], axis=-1
    )
    weights = masked_weights(jnp.concatenate([past, newer], axis=-1), mask).astype(jnp.bfloat16)
    out = jnp.einsum(
        "trkgc,rckd->trkgd",
        weights[..., :span],
        context[..., head_dim:],
        preferred_element_type=jnp.float32,
    )
    out = out + jnp.einsum(
        "trkgu,urkd->trkgd",
        weights[..., span:],
        fresh[..., head_dim:],
        preferred_element_type=jnp.float32,
    )
    return out.reshape(steps, count, width).astype(jnp.bfloat16)


def prefill_block(queries, keyvals, valid):
    slots, width = queries.shape
    kv_heads = keyvals.shape[1]
    head_dim = keyvals.shape[2] // 2
    group = width // (kv_heads * head_dim)
    scale = head_dim ** (-0.5)
    query = queries.reshape(slots, kv_heads, group, head_dim)
    block = 512
    pieces = []
    for start in range(0, slots, block):
        finish = start + block
        scores = (
            jnp.einsum(
                "qkgd,ckd->kgqc",
                query[start:finish],
                keyvals[:finish, :, :head_dim],
                preferred_element_type=jnp.float32,
            )
            * scale
        )
        query_pos = jnp.arange(start, finish, dtype=jnp.int32)
        key_pos = jnp.arange(finish, dtype=jnp.int32)
        mask = (valid[None, :finish] & (key_pos[None, :] <= query_pos[:, None]))[None, None]
        weights = masked_weights(scores, jnp.broadcast_to(mask, scores.shape)).astype(jnp.bfloat16)
        out = jnp.einsum(
            "kgqc,ckd->qkgd",
            weights,
            keyvals[:finish, :, head_dim:],
            preferred_element_type=jnp.float32,
        )
        out = jnp.where(valid[start:finish, None, None, None], out, jnp.float32(0.0))
        pieces.append(out.reshape(block, width).astype(jnp.bfloat16))
    return jnp.concatenate(pieces, axis=0)


def local(
    step_queries,
    step_keyvals,
    cache_pages,
    block_table,
    context_len,
    partner,
    moved_slot,
    prompt_queries,
    prompt_keyvals,
    prompt_target,
):
    inst_count = lax.axis_size("inst")
    tp_count = lax.axis_size("tp")
    me_inst = lax.axis_index("inst")
    me_tp = lax.axis_index("tp")
    requests = block_table.shape[0]
    kv_heads = step_keyvals.shape[2]
    head_dim = step_keyvals.shape[3] // 2
    rows_dev = prompt_queries.shape[0]
    capacity = max(2, 2 * rows_dev // inst_count)
    devices = inst_count * tp_count
    targets = prompt_target[:, 0].reshape(devices, rows_dev)
    mine = lax.dynamic_index_in_dim(targets, me_inst * tp_count + me_tp, 0, keepdims=False)
    onehot = (mine[:, None] == jnp.arange(inst_count, dtype=jnp.int32)[None, :]).astype(jnp.int32)
    rank = jnp.sum((jnp.cumsum(onehot, axis=0) - onehot) * onehot, axis=1)
    place = mine * capacity + rank
    dispatch = (
        jnp.arange(inst_count * capacity, dtype=jnp.int32)[:, None] == place[None, :]
    ).astype(jnp.bfloat16)
    send_queries = (
        jnp.dot(dispatch, prompt_queries, preferred_element_type=jnp.float32)
        .astype(jnp.bfloat16)
        .reshape(inst_count, capacity, -1)
    )
    flat_keyvals = prompt_keyvals.reshape(rows_dev, -1)
    send_keyvals = (
        jnp.dot(dispatch, flat_keyvals, preferred_element_type=jnp.float32)
        .astype(jnp.bfloat16)
        .reshape(inst_count, capacity, -1)
    )
    recv_queries, recv_keyvals = (
        lax.all_to_all(
            lax.all_to_all(send_queries, "inst", split_axis=0, concat_axis=0, tiled=True),
            "tp",
            split_axis=2,
            concat_axis=1,
            tiled=True,
        ),
        lax.all_to_all(
            lax.all_to_all(send_keyvals, "inst", split_axis=0, concat_axis=0, tiled=True),
            "tp",
            split_axis=2,
            concat_axis=1,
            tiled=True,
        ),
    )
    gathered = cache_pages[block_table]
    context = gathered.reshape(requests, -1, kv_heads, 2 * head_dim)
    lengths = lax.dynamic_slice_in_dim(context_len, me_inst * requests, requests)
    my_slot = moved_slot[me_inst]
    other = partner[me_inst]
    other_len = context_len[other * requests + moved_slot[other]]
    bit_total = inst_count.bit_length() - 1
    distance = jnp.bitwise_xor(me_inst, other)
    outgoing = lax.dynamic_index_in_dim(context, my_slot, 0, keepdims=False)
    incoming = outgoing
    for bit in range(bit_total):
        arrived = swapped(outgoing, "inst", bit)
        incoming = jnp.where(distance == 1 << bit, arrived, incoming)
    context = lax.dynamic_update_index_in_dim(context, incoming, my_slot, 0)
    lengths = lengths.at[my_slot].set(other_len)
    decode_output = decode_block(step_queries, context, lengths, step_keyvals)
    slots = inst_count * tp_count * capacity
    slot_queries = recv_queries.reshape(slots, -1)
    slot_keyvals = recv_keyvals.reshape(slots, kv_heads, 2 * head_dim)
    counts = jnp.sum((targets == me_inst).astype(jnp.int32), axis=1)
    valid = (jnp.arange(capacity, dtype=jnp.int32)[None, :] < counts[:, None]).reshape(slots)
    prefill_output = prefill_block(slot_queries, slot_keyvals, valid)
    return (decode_output, prefill_output)


def solution(mesh):
    placed = (
        P(None, "inst", "tp"),
        P(None, "inst", "tp", None),
        P("inst", None, "tp", None),
        P("inst", None),
        P(),
        P(),
        P(),
        P(("inst", "tp"), None),
        P(("inst", "tp"), None, None),
        P(),
    )
    return jax.shard_map(
        local,
        mesh=mesh,
        in_specs=placed,
        out_specs=(P(None, "inst", "tp"), P("inst", "tp")),
        check_vma=False,
    )
```

profile of v0, /device:TPU:1, one launch (start us, length us, event | category | flops | bytes accessed | tf_op | source)
XLA Modules:
  0.0 244.2 jit_solution(7322671740194920094)
XLA Ops:
  1.2 1.9 reduce.11
  6.0 20.0 %all-to-all-start = ((bf16[64,2,2048]{2,1,0:T(2,128)(2,1)}), bf16[64,2,2048]{2,1,0:T(2,128)(2,1)}, u32[]{:S(2)}, u32[]{:S(2)}) async-start(bf16[64,2,2048]{2,1,0:T(2,128)(2,1)} %reshape.492), calls=%async_computation | async-start | bytes 1048576 | tf_op jit(solution)/shard_map/all_to_all | solution.py:149
  26.6 2.6 %reshape.496 = bf16[64,2,8192]{2,1,0:T(2,128)(2,1)} reshape(bf16[128,8192]{1,0:T(8,128)(2,1)S(1)} %convolution_convert_fusion) | data formatting | bytes 4194304 | tf_op jit(solution)/shard_map/reshape | solution.py:132
  29.3 17.0 %all-to-all-done = bf16[64,2,2048]{2,1,0:T(2,128)(2,1)} async-done(((bf16[64,2,2048]{2,1,0:T(2,128)(2,1)}), bf16[64,2,2048]{2,1,0:T(2,128)(2,1)}, u32[]{:S(2)}, u32[]{:S(2)}) %all-to-all-start) | async-done | bytes 524320 | tf_op jit(solution)/shard_map/all_to_all | solution.py:149
  46.2 6.5 %all-to-all-start.2 = ((bf16[64,2,8192]{2,1,0:T(2,128)(2,1)}), bf16[64,2,8192]{2,1,0:T(2,128)(2,1)S(1)}, u32[]{:S(2)}, u32[]{:S(2)}) async-start(bf16[64,2,8192]{2,1,0:T(2,128)(2,1)} %reshape.496), calls=%async_computation.2 | async-start | bytes 4194304 | tf_op jit(solution)/shard_map/all_to_all | solution.py:142
  52.7 2.6 %copy.67 = bf16[64,2,2048]{0,1,2:T(2,128)(2,1)S(1)} copy(bf16[64,2,2048]{2,1,0:T(2,128)(2,1)} %all-to-all-done) | data formatting | bytes 1048576 | tf_op jit(solution)/shard_map/all_to_all | solution.py:149
  56.8 48.4 %all-to-all-done.2 = bf16[64,2,8192]{2,1,0:T(2,128)(2,1)S(1)} async-done(((bf16[64,2,8192]{2,1,0:T(2,128)(2,1)}), bf16[64,2,8192]{2,1,0:T(2,128)(2,1)S(1)}, u32[]{:S(2)}, u32[]{:S(2)}) %all-to-all-start.2) | async-done | bytes 2097184 | tf_op jit(solution)/shard_map/all_to_all | solution.py:142
  105.3 7.9 %all-to-all-start.1 = ((bf16[8,2,16384]{2,1,0:T(2,128)(2,1)}), bf16[8,2,16384]{2,1,0:T(2,128)(2,1)S(1)}, u32[]{:S(2)}, u32[]{:S(2)}) async-start(bf16[8,2,16384]{2,1,0:T(2,128)(2,1)} %reshape.536), calls=%async_computation.1 | async-start | bytes 1048576 | tf_op jit(solution)/shard_map/all_to_all | solution.py:148
  117.6 7.7 %copy.69 = bf16[64,2,8192]{0,1,2:T(2,128)(2,1)} copy(bf16[64,2,8192]{2,1,0:T(2,128)(2,1)S(1)} %all-to-all-done.2) | data formatting | bytes 4194304 | tf_op jit(solution)/shard_map/all_to_all | solution.py:142
  125.3 7.6 %reshape.534 = bf16[8,2,65536]{2,1,0:T(2,128)(2,1)} reshape(bf16[8192,2,64]{2,1,0:T(2,128)(2,1)} %bitcast.160) | data formatting | bytes 4194304
  132.9 5.1 %all-to-all-start.3 = ((bf16[8,2,65536]{2,1,0:T(2,128)(2,1)}), bf16[8,2,65536]{2,1,0:T(2,128)(2,1)}, u32[]{:S(2)}, u32[]{:S(2)}) async-start(bf16[8,2,65536]{2,1,0:T(2,128)(2,1)} %reshape.534), calls=%async_computation.3 | async-start | bytes 4194304 | tf_op jit(solution)/shard_map/all_to_all | solution.py:141
  138.8 1.9 gather_fusion
  140.7 3.7 %collective-permute-start = (bf16[256,1,256]{2,0,1:T(8,128)(2,1)S(1)}, bf16[256,1,256]{2,0,1:T(8,128)(2,1)S(1)}, u32[]{:S(2)}, u32[]{:S(2)}) collective-permute-start(bf16[256,1,256]{2,0,1:T(8,128)(2,1)S(1)} %dynamic-slice_bitcast_fusion), channel_id=1, source_target_pairs={{0,256},{8,264},{16,272},{24,280},{32,288},{40,296},{48,304},{56,3... | collective-permute-start | bytes 393224 | tf_op jit(solution)/shard_map/ppermute | solution.py:8
  144.4 3.3 %collective-permute-start.1 = (bf16[256,1,256]{2,0,1:T(8,128)(2,1)S(1)}, bf16[256,1,256]{2,0,1:T(8,128)(2,1)S(1)}, u32[]{:S(2)}, u32[]{:S(2)}) collective-permute-start(bf16[256,1,256]{2,0,1:T(8,128)(2,1)S(1)} %dynamic-slice_bitcast_fusion), channel_id=1, source_target_pairs={{0,128},{8,136},{16,144},{24,152},{32,160},{40,168},{48,176},{56,1... | collective-permute-start | bytes 393224 | tf_op jit(solution)/shard_map/ppermute | solution.py:8
  147.7 1.9 collective-permute-start.2
  149.7 3.7 %collective-permute-start.3 = (bf16[256,1,256]{2,0,1:T(8,128)(2,1)S(1)}, bf16[256,1,256]{2,0,1:T(8,128)(2,1)S(1)}, u32[]{:S(2)}, u32[]{:S(2)}) collective-permute-start(bf16[256,1,256]{2,0,1:T(8,128)(2,1)S(1)} %dynamic-slice_bitcast_fusion), channel_id=1, source_target_pairs={{0,32},{8,40},{16,48},{24,56},{32,0},{40,8},{48,16},{56,24},{64,96... | collective-permute-start | bytes 393224 | tf_op jit(solution)/shard_map/ppermute | solution.py:8
  153.3 4.0 %collective-permute-start.4 = (bf16[256,1,256]{2,0,1:T(8,128)(2,1)S(1)}, bf16[256,1,256]{2,0,1:T(8,128)(2,1)}, u32[]{:S(2)}, u32[]{:S(2)}) collective-permute-start(bf16[256,1,256]{2,0,1:T(8,128)(2,1)S(1)} %dynamic-slice_bitcast_fusion), channel_id=1, source_target_pairs={{0,16},{8,24},{16,0},{24,8},{32,48},{40,56},{48,32},{56,40},{64,80... | collective-permute-start | bytes 393224 | tf_op jit(solution)/shard_map/ppermute | solution.py:8
  160.2 20.3 %collective-permute-done = bf16[256,1,256]{2,0,1:T(8,128)(2,1)S(1)} collective-permute-done((bf16[256,1,256]{2,0,1:T(8,128)(2,1)S(1)}, bf16[256,1,256]{2,0,1:T(8,128)(2,1)S(1)}, u32[]{:S(2)}, u32[]{:S(2)}) %collective-permute-start) | collective-permute-done | bytes 131104 | tf_op jit(solution)/shard_map/ppermute | solution.py:8
  180.5 3.6 %collective-permute-start.5 = (bf16[256,1,256]{2,0,1:T(8,128)(2,1)S(1)}, bf16[256,1,256]{2,0,1:T(8,128)(2,1)S(1)}, u32[]{:S(2)}, u32[]{:S(2)}) collective-permute-start(bf16[256,1,256]{2,0,1:T(8,128)(2,1)S(1)} %dynamic-slice_bitcast_fusion), channel_id=1, source_target_pairs={{0,8},{8,0},{16,24},{24,16},{32,40},{40,32},{48,56},{56,48},{64,72... | collective-permute-start | bytes 393224 | tf_op jit(solution)/shard_map/ppermute | solution.py:8
  185.1 2.3 collective-permute-done.5
  189.6 3.0 %reshape.537 = bf16[2048,2,64]{2,1,0:T(2,128)(2,1)S(1)} reshape(bf16[8,2,16384]{2,1,0:T(2,128)(2,1)} %copy-done.2) | data formatting | bytes 1048576
  193.6 7.4 %reshape.535 = bf16[8192,2,64]{2,1,0:T(2,128)(2,1)} reshape(bf16[8,2,65536]{2,1,0:T(2,128)(2,1)} %all-to-all-done.3) | data formatting | bytes 4194304
  201.0 11.1 %copy.70 = bf16[64,2,8,1024]{3,1,2,0:T(2,128)(2,1)} copy(bf16[64,2,8,1024]{0,1,3,2:T(2,128)(2,1)} %bitcast.161) | data formatting | bytes 4194304 | tf_op jit(solution)/shard_map/all_to_all | solution.py:141
  212.1 4.0 %fusion.40 = (bf16[32,8,2,1024]{3,2,1,0:T(2,128)(2,1)S(1)}, bf16[32,8,2,1024]{3,2,1,0:T(2,128)(2,1)}) fusion(bf16[64,8,2,1024]{3,2,1,0:T(2,128)(2,1)} %bitcast.162), kind=kLoop, calls=%fused_computation.86 | loop fusion | bytes 4194304 | tf_op jit(solution)/shard_map/slice | solution.py:78
  218.5 2.0 fusion.5
  220.5 2.9 %fusion.10 = bf16[1,128,8,512]{3,1,2,0:T(8,128)(2,1)S(1)} fusion(f32[8,512]{1,0:T(8,128)S(1)} %compare_select_fusion.1, f32[8,512]{1,0:T(8,128)S(1)} %get-tuple-element.32, f32[512,512,8]{1,0,2:T(8,128)S(1)} %get-tuple-element.33, pred[512,512]{0,1:T(8,128)(4,1)S(1)} %fusion.24, pred[512]{0:T(512)(128)(4,1)S(1)} %copy-done.7, ...), kind=kOutput, calls=%fused_computation.22 | convolution fusion | flops 550502400 | bytes 9863680 | tf_op jit(solution)/shard_map/kgqc,ckd->qkgd/dot_general | solution.py:88
  224.0 1.7 reshape.501
  225.7 3.0 %fusion = (f32[8,512]{1,0:T(8,128)S(1)}, f32[1024,512,8]{1,0,2:T(8,128)S(1)}) fusion(pred[512,1024]{0,1:T(8,128)(4,1)S(1)} %fusion.11, bf16[512,8,128]{2,1,0:T(8,128)(2,1)S(1)} %reshape.501, bf16[1024,1,256]{2,0,1:T(8,128)(2,1)S(1)} %reshape.493), kind=kOutput, calls=%fused_computation.4 | convolution fusion | flops 1086320640 | bytes 18628608 | tf_op jit(solution)/shard_map/qkgd,ckd->kgqc/dot_general | solution.py:76
  228.7 4.2 %fusion.1 = f32[8,512]{1,0:T(8,128)S(1)} fusion(f32[1024,512,8]{1,0,2:T(8,128)S(1)} %get-tuple-element.31, f32[8,512]{1,0:T(8,128)S(1)} %get-tuple-element.30, pred[512,1024]{0,1:T(8,128)(4,1)S(1)} %fusion.11), kind=kLoop, calls=%fused_computation.5 | loop fusion | flops 20967424 | bytes 17334272 | tf_op jit(solution)/shard_map/reduce_sum | solution.py:15
  233.0 6.3 %fusion.9 = bf16[1,128,8,512]{3,1,2,0:T(8,128)(2,1)} fusion(f32[8,512]{1,0:T(8,128)S(1)} %compare_select_fusion, f32[8,512]{1,0:T(8,128)S(1)} %get-tuple-element.30, f32[1024,512,8]{1,0,2:T(8,128)S(1)} %get-tuple-element.31, pred[512,1024]{0,1:T(8,128)(4,1)S(1)} %fusion.11, pred[512]{0:T(512)(128)(4,1)S(1)} %broadcast_in_dim.121, ...), kind=kOutput, calls=%fused_computation.20 | convolution fusion | flops 1099956224 | bytes 18645504 | tf_op jit(solution)/shard_map/kgqc,ckd->qkgd/dot_general | solution.py:88
  239.3 2.3 copy.78
  241.5 2.7 %pad_maximum_fusion = bf16[1024,1024]{1,0:T(8,128)(2,1)} fusion(bf16[512,1024]{1,0:T(8,128)(2,1)} %copy.78, bf16[512,1024]{1,0:T(8,128)(2,1)S(1)} %copy.77), kind=kLoop, calls=%fused_computation.18 | loop fusion | flops 4194304 | bytes 4194304 | tf_op jit(solution)/shard_map/concatenate | solution.py:96
  (80 shorter events, 14.7 us)
Async XLA Ops:
  0.6 25.3 %copy-start = (bf16[64,8192]{1,0:T(8,128)(2,1)S(1)}, bf16[64,8192]{1,0:T(8,128)(2,1)}, u32[]{:S(2)}) copy-start(bf16[64,8192]{1,0:T(8,128)(2,1)} %param.19) | copy-start | bytes 3145732
  6.0 107.2 %copy-start.10 = (s32[64]{0:T(128)S(1)}, s32[64]{0:T(128)}, u32[]{:S(2)}) copy-start(s32[64]{0:T(128)} %param.17) | copy-start | bytes 772
  6.0 109.7 %copy-start.8 = (s32[64]{0:T(128)S(1)}, s32[64]{0:T(128)}, u32[]{:S(2)}) copy-start(s32[64]{0:T(128)} %param.18) | copy-start | bytes 772
  6.0 40.3 %all-to-all-start = ((bf16[64,2,2048]{2,1,0:T(2,128)(2,1)}), bf16[64,2,2048]{2,1,0:T(2,128)(2,1)}, u32[]{:S(2)}, u32[]{:S(2)}) async-start(bf16[64,2,2048]{2,1,0:T(2,128)(2,1)} %reshape.492), calls=%async_computation | async-start | bytes 1048576 | tf_op jit(solution)/shard_map/all_to_all | solution.py:149
  46.2 59.0 %all-to-all-start.2 = ((bf16[64,2,8192]{2,1,0:T(2,128)(2,1)}), bf16[64,2,8192]{2,1,0:T(2,128)(2,1)S(1)}, u32[]{:S(2)}, u32[]{:S(2)}) async-start(bf16[64,2,8192]{2,1,0:T(2,128)(2,1)} %reshape.496), calls=%async_computation.2 | async-start | bytes 4194304 | tf_op jit(solution)/shard_map/all_to_all | solution.py:142
  105.3 27.7 %all-to-all-start.1 = ((bf16[8,2,16384]{2,1,0:T(2,128)(2,1)}), bf16[8,2,16384]{2,1,0:T(2,128)(2,1)S(1)}, u32[]{:S(2)}, u32[]{:S(2)}) async-start(bf16[8,2,16384]{2,1,0:T(2,128)(2,1)} %reshape.536), calls=%async_computation.1 | async-start | bytes 1048576 | tf_op jit(solution)/shard_map/all_to_all | solution.py:148
  117.6 20.4 %copy-start.5 = (s32[8,16]{1,0:T(8,128)S(1)}, s32[8,16]{1,0:T(8,128)}, u32[]{:S(2)}) copy-start(s32[8,16]{1,0:T(8,128)} %param.15) | copy-start | bytes 1540
  117.6 42.0 %copy-start.4 = (bf16[4,8,1,256]{3,1,2,0:T(8,128)(2,1)S(1)}, bf16[4,8,1,256]{3,1,2,0:T(8,128)(2,1)}, u32[]{:S(2)}) copy-start(bf16[4,8,1,256]{3,1,2,0:T(8,128)(2,1)} %param.13) | copy-start | bytes 49156
  125.3 34.0 %copy-start.9 = (s32[512]{0:T(512)S(1)}, s32[512]{0:T(512)}, u32[]{:S(2)}) copy-start(s32[512]{0:T(512)} %param.16) | copy-start | bytes 6148
  125.3 59.6 %copy-start.3 = (bf16[4,8,1024]{2,1,0:T(8,128)(2,1)S(1)}, bf16[4,8,1024]{2,1,0:T(8,128)(2,1)}, u32[]{:S(2)}) copy-start(bf16[4,8,1024]{2,1,0:T(8,128)(2,1)} %param.12) | copy-start | bytes 196612
  132.9 54.5 %copy-start.2 = (bf16[8,2,16384]{2,1,0:T(2,128)(2,1)}, bf16[8,2,16384]{2,1,0:T(2,128)(2,1)S(1)}, u32[]{:S(2)}) copy-start(bf16[8,2,16384]{2,1,0:T(2,128)(2,1)S(1)} %all-to-all-done.1) | copy-start | bytes 1572868
  132.9 60.6 %all-to-all-start.3 = ((bf16[8,2,65536]{2,1,0:T(2,128)(2,1)}), bf16[8,2,65536]{2,1,0:T(2,128)(2,1)}, u32[]{:S(2)}, u32[]{:S(2)}) async-start(bf16[8,2,65536]{2,1,0:T(2,128)(2,1)} %reshape.534), calls=%async_computation.3 | async-start | bytes 4194304 | tf_op jit(solution)/shard_map/all_to_all | solution.py:141
  140.7 39.8 %collective-permute-start = (bf16[256,1,256]{2,0,1:T(8,128)(2,1)S(1)}, bf16[256,1,256]{2,0,1:T(8,128)(2,1)S(1)}, u32[]{:S(2)}, u32[]{:S(2)}) collective-permute-start(bf16[256,1,256]{2,0,1:T(8,128)(2,1)S(1)} %dynamic-slice_bitcast_fusion), channel_id=1, source_target_pairs={{0,256},{8,264},{16,272},{24,280},{32,288},{40,296},{48,304},{56,3... | collective-permute-start | bytes 393224 | tf_op jit(solution)/shard_map/ppermute | solution.py:8
  144.4 40.7 %collective-permute-start.1 = (bf16[256,1,256]{2,0,1:T(8,128)(2,1)S(1)}, bf16[256,1,256]{2,0,1:T(8,128)(2,1)S(1)}, u32[]{:S(2)}, u32[]{:S(2)}) collective-permute-start(bf16[256,1,256]{2,0,1:T(8,128)(2,1)S(1)} %dynamic-slice_bitcast_fusion), channel_id=1, source_target_pairs={{0,128},{8,136},{16,144},{24,152},{32,160},{40,168},{48,176},{56,1... | collective-permute-start | bytes 393224 | tf_op jit(solution)/shard_map/ppermute | solution.py:8
  147.7 37.3 %collective-permute-start.2 = (bf16[256,1,256]{2,0,1:T(8,128)(2,1)S(1)}, bf16[256,1,256]{2,0,1:T(8,128)(2,1)S(1)}, u32[]{:S(2)}, u32[]{:S(2)}) collective-permute-start(bf16[256,1,256]{2,0,1:T(8,128)(2,1)S(1)} %dynamic-slice_bitcast_fusion), channel_id=1, source_target_pairs={{0,64},{8,72},{16,80},{24,88},{32,96},{40,104},{48,112},{56,120},{... | collective-permute-start | bytes 393224 | tf_op jit(solution)/shard_map/ppermute | solution.py:8
  149.7 35.4 %collective-permute-start.3 = (bf16[256,1,256]{2,0,1:T(8,128)(2,1)S(1)}, bf16[256,1,256]{2,0,1:T(8,128)(2,1)S(1)}, u32[]{:S(2)}, u32[]{:S(2)}) collective-permute-start(bf16[256,1,256]{2,0,1:T(8,128)(2,1)S(1)} %dynamic-slice_bitcast_fusion), channel_id=1, source_target_pairs={{0,32},{8,40},{16,48},{24,56},{32,0},{40,8},{48,16},{56,24},{64,96... | collective-permute-start | bytes 393224 | tf_op jit(solution)/shard_map/ppermute | solution.py:8
  153.3 31.8 %collective-permute-start.4 = (bf16[256,1,256]{2,0,1:T(8,128)(2,1)S(1)}, bf16[256,1,256]{2,0,1:T(8,128)(2,1)}, u32[]{:S(2)}, u32[]{:S(2)}) collective-permute-start(bf16[256,1,256]{2,0,1:T(8,128)(2,1)S(1)} %dynamic-slice_bitcast_fusion), channel_id=1, source_target_pairs={{0,16},{8,24},{16,0},{24,8},{32,48},{40,56},{48,32},{56,40},{64,80... | collective-permute-start | bytes 393224 | tf_op jit(solution)/shard_map/ppermute | solution.py:8
  159.3 25.6 %copy-start.6 = (pred[512]{0:T(512)(128)(4,1)}, pred[512]{0:T(512)(128)(4,1)S(1)}, u32[]{:S(2)}) copy-start(pred[512]{0:T(512)(128)(4,1)S(1)} %broadcast_in_dim.114) | copy-start | bytes 1540
  180.5 7.0 %collective-permute-start.5 = (bf16[256,1,256]{2,0,1:T(8,128)(2,1)S(1)}, bf16[256,1,256]{2,0,1:T(8,128)(2,1)S(1)}, u32[]{:S(2)}, u32[]{:S(2)}) collective-permute-start(bf16[256,1,256]{2,0,1:T(8,128)(2,1)S(1)} %dynamic-slice_bitcast_fusion), channel_id=1, source_target_pairs={{0,8},{8,0},{16,24},{24,16},{32,40},{40,32},{48,56},{56,48},{64,72... | collective-permute-start | bytes 393224 | tf_op jit(solution)/shard_map/ppermute | solution.py:8
  216.8 3.7 %copy-start.7 = (pred[512]{0:T(512)(128)(4,1)S(1)}, pred[512]{0:T(512)(128)(4,1)}, u32[]{:S(2)}) copy-start(pred[512]{0:T(512)(128)(4,1)} %copy-done.6) | copy-start | bytes 1540
  233.0 11.2 %copy-start.1 = (bf16[64,8192]{1,0:T(8,128)(2,1)S(1)}, bf16[64,8192]{1,0:T(8,128)(2,1)}, u32[]{:S(2)}) copy-start(bf16[64,8192]{1,0:T(8,128)(2,1)} %param.19) | copy-start | bytes 3145732
where the time goes:
time: 246 us; the launch traced here: 244 us
  waiting for transfers between devices  88 us (36%)
  local copies, waits for them, and re-layouts  61.1 us (25%)
  starting transfers between devices  59.7 us (24%)
  matrix products  15.5 us (6%)
  other arithmetic  13 us (5%)
  between operations  6.95 us (3%)
    all_to_all x1, waiting for transfers between devices, local(): lax.all_to_all(send_queries, 'inst', split_axis=0, concat_axis=0, tiled=T...  48.4 us
    ppermute x6, waiting for transfers between devices, swapped(): lax.ppermute(array, axis, [(i, i ^ 1 << bit) for i in range(lax.axis_size...  22.6 us
    unnamed x29, local copies, waits for them, and re-layouts  21.7 us
    ppermute x6, starting transfers between devices, swapped(): lax.ppermute(array, axis, [(i, i ^ 1 << bit) for i in range(lax.axis_size...  20.2 us
    all_to_all x1, starting transfers between devices, local(): lax.all_to_all(send_keyvals, 'inst', split_axis=0, concat_axis=0, tiled=T...  20 us
    all_to_all x1, waiting for transfers between devices, local(): lax.all_to_all(send_keyvals, 'inst', split_axis=0, concat_axis=0, tiled=T...  17 us
    all_to_all x1, local copies, waits for them, and re-layouts, local(): lax.all_to_all(lax.all_to_all(send_queries, 'inst', split_axis=0, concat_...  11.1 us
    dot_general x2, matrix products, prefill_block(): jnp.einsum('kgqc,ckd->qkgd', weights, keyvals[:finish, :, head_dim:], pre...  9.18 us
  transfers between devices with their start and end apart: 10, of which 4 were waited for; matrix products, arithmetic and copies ran while one was open for 14% of the time, Pallas kernels for 0%

commit v1 on v0

--- a/solution.py
+++ b/solution.py
@@ -138,12 +138,22 @@
         .reshape(inst_count, capacity, -1)
     )
     recv_queries, recv_keyvals = (
-        lax.all_to_all(
-            lax.all_to_all(send_queries, "inst", split_axis=0, concat_axis=0, tiled=True),
-            "tp",
-            split_axis=2,
-            concat_axis=1,
-            tiled=True,
+        jnp.concatenate(
+            lax.all_to_all(
+                jnp.stack(
+                    jnp.split(
+                        lax.all_to_all(
+                            send_queries, "inst", split_axis=0, concat_axis=0, tiled=True
+                        ),
+                        lax.axis_size("tp"),
+                        axis=2,
+                    )
+                ),
+                "tp",
+                0,
+                0,
+            ),
+            axis=1,
         ),
         lax.all_to_all(
             lax.all_to_all(send_keyvals, "inst", split_axis=0, concat_axis=0, tiled=True),

time: 246 us -> 230 us (0.935)
  local copies, waits for them, and re-layouts: 61.1 us -> 45.6 us
    all_to_all x2 -> x0, local copies, waits for them, and re-layouts: 18.8 us -> none  [the longest x1 11.1 us: local(): lax.all_to_all(lax.all_to_all(send_queries, 'inst', split_axis=0, concat_...]
    all_to_all x1, waiting for transfers between devices: 48.4 us -> 40.6 us  [local(): lax.all_to_all(send_queries, 'inst', split_axis=0, concat_axis=0, tiled=T...]
    all_to_all x1, waiting for transfers between devices: 0.01 us -> 7.21 us  [local(): lax.all_to_all(lax.all_to_all(send_keyvals, 'inst', split_axis=0, concat_...]
    unnamed x29 -> x32, local copies, waits for them, and re-layouts: 21.7 us -> 15.5 us
    slice x1 -> x3, local copies, waits for them, and re-layouts: 4.03 us -> 7.71 us  [prefill_block(): query[start:finish]]
  transfers between devices with their start and end apart: 10 -> 10, of which waited for: 4 -> 5; matrix products, arithmetic and copies ran while one was open for 14% -> 14% of each run, Pallas kernels for 0% -> 0%
where the time goes in v1:
time: 230 us; the launch traced here: 229 us
  waiting for transfers between devices  86.8 us (38%)
  starting transfers between devices  59.7 us (26%)
  local copies, waits for them, and re-layouts  45.6 us (20%)
  matrix products  16.3 us (7%)
  other arithmetic  13.7 us (6%)
  between operations  6.89 us (3%)
    all_to_all x1, waiting for transfers between devices, local(): lax.all_to_all(send_queries, 'inst', split_axis=0, concat_axis=0, tiled=T...  40.6 us
    ppermute x6, waiting for transfers between devices, swapped(): lax.ppermute(array, axis, [(i, i ^ 1 << bit) for i in range(lax.axis_size...  22.1 us
    ppermute x6, starting transfers between devices, swapped(): lax.ppermute(array, axis, [(i, i ^ 1 << bit) for i in range(lax.axis_size...  20.2 us
    all_to_all x1, starting transfers between devices, local(): lax.all_to_all(send_keyvals, 'inst', split_axis=0, concat_axis=0, tiled=T...  19.8 us
    all_to_all x1, waiting for transfers between devices, local(): lax.all_to_all(send_keyvals, 'inst', split_axis=0, concat_axis=0, tiled=T...  16.9 us
    unnamed x32, local copies, waits for them, and re-layouts  15.5 us
    dot_general x2, matrix products, prefill_block(): jnp.einsum('kgqc,ckd->qkgd', weights, keyvals[:finish, :, head_dim:], pre...  10 us
    all_to_all x1, starting transfers between devices, local(): lax.all_to_all(lax.all_to_all(send_keyvals, 'inst', split_axis=0, concat_...  8.19 us
  transfers between devices with their start and end apart: 10, of which 5 were waited for; matrix products, arithmetic and copies ran while one was open for 14% of the time, Pallas kernels for 0%

profile of v1, /device:TPU:1, one launch (start us, length us, event | category | flops | bytes accessed | tf_op | source)
XLA Modules:
  0.0 229.0 jit_solution(15939527978129002294)
XLA Ops:
  6.0 19.8 %all-to-all-start = ((bf16[64,2,2048]{2,1,0:T(2,128)(2,1)}), bf16[64,2,2048]{2,1,0:T(2,128)(2,1)}, u32[]{:S(2)}, u32[]{:S(2)}) async-start(bf16[64,2,2048]{2,1,0:T(2,128)(2,1)} %reshape.494), calls=%async_computation | async-start | bytes 1048576 | tf_op jit(solution)/shard_map/all_to_all | solution.py:159
  26.5 2.6 %reshape.498 = bf16[64,2,8192]{2,1,0:T(2,128)(2,1)} reshape(bf16[128,8192]{1,0:T(8,128)(2,1)S(1)} %convolution_convert_fusion) | data formatting | bytes 4194304 | tf_op jit(solution)/shard_map/reshape | solution.py:132
  29.1 16.9 %all-to-all-done = bf16[64,2,2048]{2,1,0:T(2,128)(2,1)} async-done(((bf16[64,2,2048]{2,1,0:T(2,128)(2,1)}), bf16[64,2,2048]{2,1,0:T(2,128)(2,1)}, u32[]{:S(2)}, u32[]{:S(2)}) %all-to-all-start) | async-done | bytes 524320 | tf_op jit(solution)/shard_map/all_to_all | solution.py:159
  46.1 6.4 %all-to-all-start.2 = ((bf16[64,2,8192]{2,1,0:T(2,128)(2,1)}), bf16[64,2,8192]{2,1,0:T(2,128)(2,1)S(1)}, u32[]{:S(2)}, u32[]{:S(2)}) async-start(bf16[64,2,8192]{2,1,0:T(2,128)(2,1)} %reshape.498), calls=%async_computation.2 | async-start | bytes 4194304 | tf_op jit(solution)/shard_map/all_to_all | solution.py:145
  56.9 3.7 %copy.74 = bf16[64,2,2048]{0,1,2:T(2,128)(2,1)} copy(bf16[64,2,2048]{2,1,0:T(2,128)(2,1)} %all-to-all-done) | data formatting | bytes 1048576 | tf_op jit(solution)/shard_map/all_to_all | solution.py:159
  60.7 3.8 %reshape.537 = bf16[8,2,16384]{2,1,0:T(2,128)(2,1)} reshape(bf16[2048,2,64]{2,1,0:T(2,128)(2,1)} %bitcast.189) | data formatting | bytes 1048576
  64.5 40.6 %all-to-all-done.2 = bf16[64,2,8192]{2,1,0:T(2,128)(2,1)S(1)} async-done(((bf16[64,2,8192]{2,1,0:T(2,128)(2,1)}), bf16[64,2,8192]{2,1,0:T(2,128)(2,1)S(1)}, u32[]{:S(2)}, u32[]{:S(2)}) %all-to-all-start.2) | async-done | bytes 2097184 | tf_op jit(solution)/shard_map/all_to_all | solution.py:145
  105.1 8.2 %all-to-all-start.1 = ((bf16[8,2,16384]{2,1,0:T(2,128)(2,1)}), bf16[8,2,16384]{2,1,0:T(2,128)(2,1)}, u32[]{:S(2)}, u32[]{:S(2)}) async-start(bf16[8,2,16384]{2,1,0:T(2,128)(2,1)} %reshape.537), calls=%async_computation.1 | async-start | bytes 1048576 | tf_op jit(solution)/shard_map/all_to_all | solution.py:158
  120.7 7.2 %all-to-all-done.1 = bf16[8,2,16384]{2,1,0:T(2,128)(2,1)} async-done(((bf16[8,2,16384]{2,1,0:T(2,128)(2,1)}), bf16[8,2,16384]{2,1,0:T(2,128)(2,1)}, u32[]{:S(2)}, u32[]{:S(2)}) %all-to-all-start.1) | async-done | bytes 524320 | tf_op jit(solution)/shard_map/all_to_all | solution.py:158
  127.9 5.1 %all-to-all-start.3 = ((bf16[8,64,2,1024]{3,2,1,0:T(2,128)(2,1)}), bf16[8,64,2,1024]{3,2,1,0:T(2,128)(2,1)}, u32[]{:S(2)}, u32[]{:S(2)}) async-start(bf16[8,64,2,1024]{3,2,1,0:T(2,128)(2,1)} %fusion.25), calls=%async_computation.3 | async-start | bytes 4194304 | tf_op jit(solution)/shard_map/all_to_all | solution.py:142
  133.7 1.9 gather_fusion
  135.6 3.3 %collective-permute-start = (bf16[256,1,256]{2,0,1:T(8,128)(2,1)S(1)}, bf16[256,1,256]{2,0,1:T(8,128)(2,1)S(1)}, u32[]{:S(2)}, u32[]{:S(2)}) collective-permute-start(bf16[256,1,256]{2,0,1:T(8,128)(2,1)S(1)} %dynamic-slice_bitcast_fusion), channel_id=1, source_target_pairs={{0,256},{8,264},{16,272},{24,280},{32,288},{40,296},{48,304},{56,3... | collective-permute-start | bytes 393224 | tf_op jit(solution)/shard_map/ppermute | solution.py:8
  138.9 3.3 %collective-permute-start.1 = (bf16[256,1,256]{2,0,1:T(8,128)(2,1)S(1)}, bf16[256,1,256]{2,0,1:T(8,128)(2,1)}, u32[]{:S(2)}, u32[]{:S(2)}) collective-permute-start(bf16[256,1,256]{2,0,1:T(8,128)(2,1)S(1)} %dynamic-slice_bitcast_fusion), channel_id=1, source_target_pairs={{0,128},{8,136},{16,144},{24,152},{32,160},{40,168},{48,176},{56,1... | collective-permute-start | bytes 393224 | tf_op jit(solution)/shard_map/ppermute | solution.py:8
  142.2 2.0 collective-permute-start.2
  144.2 4.3 %collective-permute-start.3 = (bf16[256,1,256]{2,0,1:T(8,128)(2,1)S(1)}, bf16[256,1,256]{2,0,1:T(8,128)(2,1)}, u32[]{:S(2)}, u32[]{:S(2)}) collective-permute-start(bf16[256,1,256]{2,0,1:T(8,128)(2,1)S(1)} %dynamic-slice_bitcast_fusion), channel_id=1, source_target_pairs={{0,32},{8,40},{16,48},{24,56},{32,0},{40,8},{48,16},{56,24},{64,96... | collective-permute-start | bytes 393224 | tf_op jit(solution)/shard_map/ppermute | solution.py:8
  148.5 3.6 %collective-permute-start.4 = (bf16[256,1,256]{2,0,1:T(8,128)(2,1)S(1)}, bf16[256,1,256]{2,0,1:T(8,128)(2,1)}, u32[]{:S(2)}, u32[]{:S(2)}) collective-permute-start(bf16[256,1,256]{2,0,1:T(8,128)(2,1)S(1)} %dynamic-slice_bitcast_fusion), channel_id=1, source_target_pairs={{0,16},{8,24},{16,0},{24,8},{32,48},{40,56},{48,32},{56,40},{64,80... | collective-permute-start | bytes 393224 | tf_op jit(solution)/shard_map/ppermute | solution.py:8
  154.9 20.1 %collective-permute-done = bf16[256,1,256]{2,0,1:T(8,128)(2,1)S(1)} collective-permute-done((bf16[256,1,256]{2,0,1:T(8,128)(2,1)S(1)}, bf16[256,1,256]{2,0,1:T(8,128)(2,1)S(1)}, u32[]{:S(2)}, u32[]{:S(2)}) %collective-permute-start) | collective-permute-done | bytes 131104 | tf_op jit(solution)/shard_map/ppermute | solution.py:8
  175.0 3.8 %collective-permute-start.5 = (bf16[256,1,256]{2,0,1:T(8,128)(2,1)S(1)}, bf16[256,1,256]{2,0,1:T(8,128)(2,1)S(1)}, u32[]{:S(2)}, u32[]{:S(2)}) collective-permute-start(bf16[256,1,256]{2,0,1:T(8,128)(2,1)S(1)} %dynamic-slice_bitcast_fusion), channel_id=1, source_target_pairs={{0,8},{8,0},{16,24},{24,16},{32,40},{40,32},{48,56},{56,48},{64,72... | collective-permute-start | bytes 393224 | tf_op jit(solution)/shard_map/ppermute | solution.py:8
  179.8 1.9 collective-permute-done.5
  184.8 3.0 %reshape.538 = bf16[2048,2,64]{2,1,0:T(2,128)(2,1)S(1)} reshape(bf16[8,2,16384]{2,1,0:T(2,128)(2,1)} %all-to-all-done.1) | data formatting | bytes 1048576
  189.6 3.5 %fusion.48 = (bf16[32,8,2,1024]{3,2,0,1:T(2,128)(2,1)S(1)}, bf16[32,8,2,1024]{3,2,0,1:T(2,128)(2,1)}) fusion(bf16[64,8,2,1024]{3,2,0,1:T(2,128)(2,1)} %bitcast.47), kind=kLoop, calls=%fused_computation.102 | loop fusion | bytes 4194304 | tf_op jit(solution)/shard_map/slice | solution.py:78
  193.1 2.1 copy.76
  198.6 2.0 fusion.5
  200.6 3.7 %fusion.10 = bf16[1,128,8,512]{3,1,2,0:T(8,128)(2,1)} fusion(f32[8,512]{1,0:T(8,128)S(1)} %compare_select_fusion.1, f32[8,512]{1,0:T(8,128)S(1)} %get-tuple-element.32, f32[512,512,8]{1,0,2:T(8,128)S(1)} %get-tuple-element.33, pred[512,512]{0,1:T(8,128)(4,1)S(1)} %fusion.24, pred[512]{0:T(512)(128)(4,1)S(1)} %broadcast_in_dim.114, ...), kind=kOutput, calls=%fused_computation.22 | convolution fusion | flops 550502400 | bytes 9863680 | tf_op jit(solution)/shard_map/kgqc,ckd->qkgd/dot_general | solution.py:88
  204.4 2.3 copy.84
  206.6 2.1 copy.80
  208.7 2.0 reshape.504
  210.7 3.0 %fusion = (f32[8,512]{1,0:T(8,128)S(1)}, f32[1024,512,8]{1,0,2:T(8,128)S(1)}) fusion(pred[512,1024]{0,1:T(8,128)(4,1)S(1)} %fusion.11, bf16[512,8,128]{2,1,0:T(8,128)(2,1)S(1)} %reshape.504, bf16[1024,1,256]{2,0,1:T(8,128)(2,1)S(1)} %copy-done.3), kind=kOutput, calls=%fused_computation.4 | convolution fusion | flops 1086320640 | bytes 18628608 | tf_op jit(solution)/shard_map/qkgd,ckd->kgqc/dot_general | solution.py:76
  213.7 4.0 %fusion.1 = f32[8,512]{1,0:T(8,128)S(1)} fusion(f32[1024,512,8]{1,0,2:T(8,128)S(1)} %get-tuple-element.31, f32[8,512]{1,0:T(8,128)S(1)} %get-tuple-element.30, pred[512,1024]{0,1:T(8,128)(4,1)S(1)} %fusion.11), kind=kLoop, calls=%fused_computation.5 | loop fusion | flops 20967424 | bytes 17334272 | tf_op jit(solution)/shard_map/reduce_sum | solution.py:15
  217.7 6.3 %fusion.9 = bf16[1,128,8,512]{3,1,2,0:T(8,128)(2,1)} fusion(f32[8,512]{1,0:T(8,128)S(1)} %compare_select_fusion, f32[8,512]{1,0:T(8,128)S(1)} %get-tuple-element.30, f32[1024,512,8]{1,0,2:T(8,128)S(1)} %get-tuple-element.31, pred[512,1024]{0,1:T(8,128)(4,1)S(1)} %fusion.11, pred[512]{0:T(512)(128)(4,1)S(1)} %broadcast_in_dim.121, ...), kind=kOutput, calls=%fused_computation.20 | convolution fusion | flops 1099956224 | bytes 18645504 | tf_op jit(solution)/shard_map/kgqc,ckd->qkgd/dot_general | solution.py:88
  224.0 2.3 copy.85
  226.3 2.7 %pad_maximum_fusion = bf16[1024,1024]{1,0:T(8,128)(2,1)} fusion(bf16[512,1024]{1,0:T(8,128)(2,1)} %copy.85, bf16[512,1024]{1,0:T(8,128)(2,1)S(1)} %copy-done.1), kind=kLoop, calls=%fused_computation.18 | loop fusion | flops 4194304 | bytes 4194304 | tf_op jit(solution)/shard_map/concatenate | solution.py:96
  (84 shorter events, 24.6 us)
Async XLA Ops:
  0.6 25.2 %copy-start = (bf16[64,8192]{1,0:T(8,128)(2,1)S(1)}, bf16[64,8192]{1,0:T(8,128)(2,1)}, u32[]{:S(2)}) copy-start(bf16[64,8192]{1,0:T(8,128)(2,1)} %param.19) | copy-start | bytes 3145732
  6.0 40.1 %all-to-all-start = ((bf16[64,2,2048]{2,1,0:T(2,128)(2,1)}), bf16[64,2,2048]{2,1,0:T(2,128)(2,1)}, u32[]{:S(2)}, u32[]{:S(2)}) async-start(bf16[64,2,2048]{2,1,0:T(2,128)(2,1)} %reshape.494), calls=%async_computation | async-start | bytes 1048576 | tf_op jit(solution)/shard_map/all_to_all | solution.py:159
  26.5 26.0 %copy-start.9 = (s32[64]{0:T(128)S(1)}, s32[64]{0:T(128)}, u32[]{:S(2)}) copy-start(s32[64]{0:T(128)} %param.17) | copy-start | bytes 772
  26.5 28.5 %copy-start.7 = (s32[64]{0:T(128)S(1)}, s32[64]{0:T(128)}, u32[]{:S(2)}) copy-start(s32[64]{0:T(128)} %param.18) | copy-start | bytes 772
  46.1 59.0 %all-to-all-start.2 = ((bf16[64,2,8192]{2,1,0:T(2,128)(2,1)}), bf16[64,2,8192]{2,1,0:T(2,128)(2,1)S(1)}, u32[]{:S(2)}, u32[]{:S(2)}) async-start(bf16[64,2,8192]{2,1,0:T(2,128)(2,1)} %reshape.498), calls=%async_computation.2 | async-start | bytes 4194304 | tf_op jit(solution)/shard_map/all_to_all | solution.py:145
  105.1 22.8 %all-to-all-start.1 = ((bf16[8,2,16384]{2,1,0:T(2,128)(2,1)}), bf16[8,2,16384]{2,1,0:T(2,128)(2,1)}, u32[]{:S(2)}, u32[]{:S(2)}) async-start(bf16[8,2,16384]{2,1,0:T(2,128)(2,1)} %reshape.537), calls=%async_computation.1 | async-start | bytes 1048576 | tf_op jit(solution)/shard_map/all_to_all | solution.py:158
  113.2 19.7 %copy-start.6 = (s32[8,16]{1,0:T(8,128)S(1)}, s32[8,16]{1,0:T(8,128)}, u32[]{:S(2)}) copy-start(s32[8,16]{1,0:T(8,128)} %param.15) | copy-start | bytes 1540
  118.8 35.2 %copy-start.8 = (s32[512]{0:T(512)S(1)}, s32[512]{0:T(512)}, u32[]{:S(2)}) copy-start(s32[512]{0:T(512)} %param.16) | copy-start | bytes 6148
  118.8 35.5 %copy-start.5 = (bf16[4,8,1,256]{3,1,2,0:T(8,128)(2,1)S(1)}, bf16[4,8,1,256]{3,1,2,0:T(8,128)(2,1)}, u32[]{:S(2)}) copy-start(bf16[4,8,1,256]{3,1,2,0:T(8,128)(2,1)} %param.13) | copy-start | bytes 49156
  119.7 59.9 %copy-start.4 = (bf16[4,8,1024]{2,1,0:T(8,128)(2,1)S(1)}, bf16[4,8,1024]{2,1,0:T(8,128)(2,1)}, u32[]{:S(2)}) copy-start(bf16[4,8,1024]{2,1,0:T(8,128)(2,1)} %param.12) | copy-start | bytes 196612
  127.9 61.7 %all-to-all-start.3 = ((bf16[8,64,2,1024]{3,2,1,0:T(2,128)(2,1)}), bf16[8,64,2,1024]{3,2,1,0:T(2,128)(2,1)}, u32[]{:S(2)}, u32[]{:S(2)}) async-start(bf16[8,64,2,1024]{3,2,1,0:T(2,128)(2,1)} %fusion.25), calls=%async_computation.3 | async-start | bytes 4194304 | tf_op jit(solution)/shard_map/all_to_all | solution.py:142
  135.6 39.4 %collective-permute-start = (bf16[256,1,256]{2,0,1:T(8,128)(2,1)S(1)}, bf16[256,1,256]{2,0,1:T(8,128)(2,1)S(1)}, u32[]{:S(2)}, u32[]{:S(2)}) collective-permute-start(bf16[256,1,256]{2,0,1:T(8,128)(2,1)S(1)} %dynamic-slice_bitcast_fusion), channel_id=1, source_target_pairs={{0,256},{8,264},{16,272},{24,280},{32,288},{40,296},{48,304},{56,3... | collective-permute-start | bytes 393224 | tf_op jit(solution)/shard_map/ppermute | solution.py:8
  138.9 40.8 %collective-permute-start.1 = (bf16[256,1,256]{2,0,1:T(8,128)(2,1)S(1)}, bf16[256,1,256]{2,0,1:T(8,128)(2,1)}, u32[]{:S(2)}, u32[]{:S(2)}) collective-permute-start(bf16[256,1,256]{2,0,1:T(8,128)(2,1)S(1)} %dynamic-slice_bitcast_fusion), channel_id=1, source_target_pairs={{0,128},{8,136},{16,144},{24,152},{32,160},{40,168},{48,176},{56,1... | collective-permute-start | bytes 393224 | tf_op jit(solution)/shard_map/ppermute | solution.py:8
  142.2 37.5 %collective-permute-start.2 = (bf16[256,1,256]{2,0,1:T(8,128)(2,1)S(1)}, bf16[256,1,256]{2,0,1:T(8,128)(2,1)}, u32[]{:S(2)}, u32[]{:S(2)}) collective-permute-start(bf16[256,1,256]{2,0,1:T(8,128)(2,1)S(1)} %dynamic-slice_bitcast_fusion), channel_id=1, source_target_pairs={{0,64},{8,72},{16,80},{24,88},{32,96},{40,104},{48,112},{56,120},{... | collective-permute-start | bytes 393224 | tf_op jit(solution)/shard_map/ppermute | solution.py:8
  144.2 35.6 %collective-permute-start.3 = (bf16[256,1,256]{2,0,1:T(8,128)(2,1)S(1)}, bf16[256,1,256]{2,0,1:T(8,128)(2,1)}, u32[]{:S(2)}, u32[]{:S(2)}) collective-permute-start(bf16[256,1,256]{2,0,1:T(8,128)(2,1)S(1)} %dynamic-slice_bitcast_fusion), channel_id=1, source_target_pairs={{0,32},{8,40},{16,48},{24,56},{32,0},{40,8},{48,16},{56,24},{64,96... | collective-permute-start | bytes 393224 | tf_op jit(solution)/shard_map/ppermute | solution.py:8
  148.5 31.3 %collective-permute-start.4 = (bf16[256,1,256]{2,0,1:T(8,128)(2,1)S(1)}, bf16[256,1,256]{2,0,1:T(8,128)(2,1)}, u32[]{:S(2)}, u32[]{:S(2)}) collective-permute-start(bf16[256,1,256]{2,0,1:T(8,128)(2,1)S(1)} %dynamic-slice_bitcast_fusion), channel_id=1, source_target_pairs={{0,16},{8,24},{16,0},{24,8},{32,48},{40,56},{48,32},{56,40},{64,80... | collective-permute-start | bytes 393224 | tf_op jit(solution)/shard_map/ppermute | solution.py:8
  175.0 6.7 %collective-permute-start.5 = (bf16[256,1,256]{2,0,1:T(8,128)(2,1)S(1)}, bf16[256,1,256]{2,0,1:T(8,128)(2,1)S(1)}, u32[]{:S(2)}, u32[]{:S(2)}) collective-permute-start(bf16[256,1,256]{2,0,1:T(8,128)(2,1)S(1)} %dynamic-slice_bitcast_fusion), channel_id=1, source_target_pairs={{0,8},{8,0},{16,24},{24,16},{32,40},{40,32},{48,56},{56,48},{64,72... | collective-permute-start | bytes 393224 | tf_op jit(solution)/shard_map/ppermute | solution.py:8
  189.6 7.4 %copy-start.3 = (bf16[1024,1,256]{2,0,1:T(8,128)(2,1)S(1)}, bf16[1024,1,256]{2,0,1:T(8,128)(2,1)}, u32[]{:S(2)}) copy-start(bf16[1024,1,256]{2,0,1:T(8,128)(2,1)} %reshape.495) | copy-start | bytes 1572868
  200.6 6.0 %copy-start.2 = (bf16[32,8,2,1024]{3,2,0,1:T(2,128)(2,1)S(1)}, bf16[32,8,2,1024]{3,2,0,1:T(2,128)(2,1)}, u32[]{:S(2)}) copy-start(bf16[32,8,2,1024]{3,2,0,1:T(2,128)(2,1)} %get-tuple-element.23) | copy-start | bytes 3145732
  217.7 8.6 %copy-start.1 = (bf16[512,1024]{1,0:T(8,128)(2,1)S(1)}, bf16[512,1024]{1,0:T(8,128)(2,1)}, u32[]{:S(2)}) copy-start(bf16[512,1024]{1,0:T(8,128)(2,1)} %copy.84) | copy-start | bytes 3145732
